TPU v7x, 32 devices: a whole 2x2x4 slice. The times are simulated.
32 devices in a mesh: dom: 4 (over y, x), head: 8 (over z, core).
Axes of the slice: x: 2, y: 2, z: 4, core: 2. Of those that a mesh axis runs over, the one named last changes fastest.
Arguments:
- node_queries: bfloat16 [8192, 1024], P(('dom', 'head')), may hold values from -20 to 20
- node_keys: bfloat16 [8192, 1024], P(('dom', 'head')), may hold values from -20 to 20
- node_values: bfloat16 [8192, 1024], P(('dom', 'head')), may hold values from -6 to 6
- out_grad: bfloat16 [8192, 1024], P(('dom', 'head')), may hold values from -6 to 6
- degrees: int32 [8192], P('dom'), may hold values from 8 to 4096
- neighbor_blocks: int32 [64, 12], P('dom'), may hold values from 0 to 31, as said below
- send_slots: int32 [4, 4, 4], replicated, may hold values from -1 to 15, as said below
Outputs:
- grad_queries: bfloat16 [8192, 1024], P(('dom', 'head'))
- grad_keys: bfloat16 [8192, 1024], P(('dom', 'head'))
- grad_values: bfloat16 [8192, 1024], P(('dom', 'head'))
Inputs may be any that keep to these rules, and one draw needn't show every extreme that they name: `neighbor_blocks`: an entry t below 16 names block t of the row's own partition; entry 16 + q * 4 + s names slot s of send_slots[q, p] for the row's partition p, and that slot is live. The 12 entries of a row are distinct, and every live slot listed for a partition is named by some row block of it. send_slots[q, p] holds distinct local block numbers of partition q, live slots first and -1 in empty ones; send_slots[p, p] is empty; for every destination p at least one source fills all 4 slots, every other source fills 1 to 4.
All inputs are finite; a program needn't handle non-finite values.
Results may differ from a plain program's by a relative error of at most 0.0068.
Values may be sent and summed in bfloat16 or wider, within the bound.
No kernel may reach another device: no remote copies, remote signals or barrier semaphores. Data moves between devices by JAX's collectives and lax.ppermute only.
A program may use at most 128 MiB of HBM per device.

v0:
```python
import math
import jax
import jax.numpy as jnp
from jax import lax
from jax.sharding import PartitionSpec as P

D = 1024
H = 16
NBR = 12
BS = 128


def borrow_table(keys_h, values_h, my_lists, block):
    rows, width = keys_h.shape
    nblk = rows // block
    kv_local = jnp.concatenate([keys_h, values_h], 1).reshape(nblk, block, 2 * width)
    outgoing = jnp.take(kv_local, jnp.maximum(my_lists, 0).reshape(-1), axis=0)
    borrowed = lax.all_to_all(outgoing, "dom", split_axis=0, concat_axis=0, tiled=True)
    return jnp.concatenate([kv_local, borrowed], 0)


def body(node_queries, node_keys, node_values, out_grad, degrees, neighbor_blocks, send_slots):
    head_dim = D // H
    block = BS
    heads_here = H // lax.axis_size("head")
    parts = lax.axis_size("dom")
    my_lists = lax.dynamic_index_in_dim(send_slots, lax.axis_index("dom"), 0, keepdims=False)
    queries, keys_h, values_h, grads_h = (
        lax.all_to_all(node_queries, "head", split_axis=1, concat_axis=0, tiled=True),
        lax.all_to_all(node_keys, "head", split_axis=1, concat_axis=0, tiled=True),
        lax.all_to_all(node_values, "head", split_axis=1, concat_axis=0, tiled=True),
        lax.all_to_all(out_grad, "head", split_axis=1, concat_axis=0, tiled=True),
    )
    table = borrow_table(keys_h, values_h, my_lists, block)
    rows, width = queries.shape
    nblk = rows // block
    scale_rows = jnp.log(degrees.astype(jnp.float32)) / math.log(64.0) / math.sqrt(head_dim)
    group_rows = 4 * block
    span = NBR * block

    def group(acc, index):
        start = index * group_rows
        queries_g = lax.dynamic_slice_in_dim(queries, start, group_rows, 0).reshape(4, block, width)
        grads_g = lax.dynamic_slice_in_dim(grads_h, start, group_rows, 0).reshape(4, block, width)
        scale = lax.dynamic_slice_in_dim(scale_rows, start, group_rows, 0).reshape(4, block, 1)
        picks = lax.dynamic_slice_in_dim(neighbor_blocks, index * 4, 4, 0).reshape(-1)
        gathered = jnp.take(table, picks, axis=0).reshape(4, span, 2 * width)
        grad_q_heads = []
        grad_k_heads = []
        grad_v_heads = []
        for head in range(heads_here):
            low = head * head_dim
            keys_n = gathered[:, :, low : low + head_dim]
            values_n = gathered[:, :, width + low : width + low + head_dim]
            query_one = queries_g[:, :, low : low + head_dim]
            grad_one = grads_g[:, :, low : low + head_dim]
            scores = (
                jnp.einsum("gid,gjd->gij", query_one, keys_n, preferred_element_type=jnp.float32)
                * scale
            )
            top = jnp.max(scores, axis=-1, keepdims=True)
            expo = jnp.exp(scores - top)
            probs = expo / jnp.sum(expo, axis=-1, keepdims=True)
            dprobs = jnp.einsum(
                "gid,gjd->gij", grad_one, values_n, preferred_element_type=jnp.float32
            )
            delta = jnp.sum(probs * dprobs, axis=-1, keepdims=True)
            dscores = (probs * (dprobs - delta) * scale).astype(jnp.bfloat16)
            probs_b = probs.astype(jnp.bfloat16)
            grad_q_heads.append(
                jnp.einsum("gij,gjd->gid", dscores, keys_n, preferred_element_type=jnp.float32)
            )
            grad_k_heads.append(
                jnp.einsum("gij,gid->gjd", dscores, query_one, preferred_element_type=jnp.float32)
            )
            grad_v_heads.append(
                jnp.einsum("gij,gid->gjd", probs_b, grad_one, preferred_element_type=jnp.float32)
            )
        grad_q = jnp.concatenate(grad_q_heads, -1)
        contrib = jnp.concatenate(grad_k_heads + grad_v_heads, -1).reshape(
            4 * NBR, block, 2 * width
        )
        acc = acc.at[picks].add(contrib)
        return (acc, grad_q.reshape(group_rows, width).astype(jnp.bfloat16))

    acc0 = jnp.zeros((table.shape[0], block, 2 * width), jnp.float32)
    acc, grad_rows = lax.scan(group, acc0, jnp.arange(nblk // 4, dtype=jnp.int32))
    grad_queries_h = grad_rows.reshape(rows, width)
    remote = acc[nblk:].astype(jnp.bfloat16)
    returned = lax.all_to_all(remote, "dom", split_axis=0, concat_axis=0, tiled=True)
    targets = jnp.maximum(my_lists, 0).reshape(-1)
    onehot = (jnp.arange(nblk, dtype=jnp.int32)[:, None] == targets[None, :]).astype(jnp.bfloat16)
    added = jnp.dot(
        onehot, returned.reshape(parts * my_lists.shape[1], -1), preferred_element_type=jnp.float32
    )
    total = (acc[:nblk] + added.reshape(nblk, block, 2 * width)).astype(jnp.bfloat16)
    grad_keys_h = total[:, :, :width].reshape(rows, width)
    grad_values_h = total[:, :, width:].reshape(rows, width)
    grad_queries, grad_keys, grad_values = (
        lax.all_to_all(grad_queries_h, "head", split_axis=0, concat_axis=1, tiled=True),
        lax.all_to_all(grad_keys_h, "head", split_axis=0, concat_axis=1, tiled=True),
        lax.all_to_all(grad_values_h, "head", split_axis=0, concat_axis=1, tiled=True),
    )
    return (grad_queries, grad_keys, grad_values)


def solution(mesh):
    placed = (
        P(("dom", "head"), None),
        P(("dom", "head"), None),
        P(("dom", "head"), None),
        P(("dom", "head"), None),
        P("dom"),
        P("dom", None),
        P(),
    )
    return jax.shard_map(
        body,
        mesh=mesh,
        in_specs=placed,
        out_specs=(P(("dom", "head"), None), P(("dom", "head"), None), P(("dom", "head"), None)),
        check_vma=False,
    )
```

profile of v0, /device:TPU:0, one launch (start us, length us, event | category | flops | bytes accessed | tf_op | source)
XLA Modules:
  0.0 532.4 jit_solution(8709490764186849700)
XLA Ops:
  10.8 13.4 %all-to-all-done.1 = bf16[256,8,128]{2,0,1:T(8,128)(2,1)S(1)} async-done(((bf16[256,8,128]{2,0,1:T(8,128)(2,1)}), bf16[256,8,128]{2,0,1:T(8,128)(2,1)S(1)}, u32[]{:S(2)}, u32[]{:S(2)}) %all-to-all-start.1) | async-done | bytes 524320 | tf_op jit(solution)/shard_map/all_to_all | solution.py:30
  28.7 14.4 %all-to-all-done.2 = bf16[256,8,128]{2,0,1:T(8,128)(2,1)S(1)} async-done(((bf16[256,8,128]{2,0,1:T(8,128)(2,1)}), bf16[256,8,128]{2,0,1:T(8,128)(2,1)S(1)}, u32[]{:S(2)}, u32[]{:S(2)}) %all-to-all-start.2) | async-done | bytes 524320 | tf_op jit(solution)/shard_map/all_to_all | solution.py:31
  50.4 12.2 %all-to-all-done = bf16[256,8,128]{2,0,1:T(8,128)(2,1)} async-done(((bf16[256,8,128]{2,0,1:T(8,128)(2,1)}), bf16[256,8,128]{2,0,1:T(8,128)(2,1)}, u32[]{:S(2)}, u32[]{:S(2)}) %all-to-all-start) | async-done | bytes 524320 | tf_op jit(solution)/shard_map/all_to_all | solution.py:29
  67.2 12.6 %all-to-all-done.3 = bf16[16,128,256]{2,1,0:T(8,128)(2,1)S(1)} async-done(((bf16[16,128,256]{2,1,0:T(8,128)(2,1)}), bf16[16,128,256]{2,1,0:T(8,128)(2,1)S(1)}, u32[]{:S(2)}, u32[]{:S(2)}) %all-to-all-start.3) | async-done | bytes 1048608 | tf_op jit(solution)/shard_map/all_to_all | solution.py:18
  85.4 13.9 %all-to-all-done.4 = bf16[256,8,128]{2,0,1:T(8,128)(2,1)} async-done(((bf16[256,8,128]{2,0,1:T(8,128)(2,1)}), bf16[256,8,128]{2,0,1:T(8,128)(2,1)}, u32[]{:S(2)}, u32[]{:S(2)}) %all-to-all-start.4) | async-done | bytes 524320 | tf_op jit(solution)/shard_map/all_to_all | solution.py:32
  101.7 354.8 %while.12 = (s32[]{:T(128)}, f32[32,128,256]{2,1,0:T(8,128)}, bf16[4,512,128]{2,1,0:T(8,128)(2,1)}, s32[4]{0:T(128)S(1)}, s32[16,12]{1,0:T(8,128)}, /*index=5*/b...) while((s32[]{:T(128)}, f32[32,128,256]{2,1,0:T(8,128)}, ...), condition=%wide.region_8.9_spmd, body=%wide.region_0.8_spmd.sunk | while | flops 1044722112 | bytes 177150128 | solution.py:87
  123.5 7.1 %fusion.165 = bf16[4,128,64]{1,2,0:T(8,128)(2,1)S(1)} fusion(f32[4,128,1536]{2,1,0:T(8,128)} %fusion.162, f32[4,128]{1,0:T(4,128)S(1)} %dynamic-slice_bitcast_fusion.2, bf16[4,1536,256]{1,2,0:T(8,128)(2,1)} %copy-done.2, f32[4,128,1536]{2,1,0:T(8,128)} %get-tuple-element.159, f32[4,128]{1,0:T(4,128)S(1)} %get-tuple-element.160), kind=kOutput, calls=%fused_computation.41.clone.1 | convolution fusion | flops 106203136 | bytes 13441024 | tf_op jit(solution)/shard_map/while/body/eval_jaxpr/gij,gjd->gid/dot_general | solution.py:71
  130.6 8.5 %fusion.163 = f32[4,1536,64]{1,2,0:T(8,128)} fusion(f32[4,128,1536]{2,1,0:T(8,128)} %fusion.162, f32[4,128]{1,0:T(4,128)S(1)} %dynamic-slice_bitcast_fusion.2, bf16[4,128,128]{2,1,0:T(8,128)(2,1)S(1)} %bitcast.109, f32[4,128,1536]{2,1,0:T(8,128)} %get-tuple-element.159, f32[4,128]{1,0:T(4,128)S(1)} %get-tuple-element.160), kind=kOutput, calls=%fused_computation.30.clone.1 | convolution fusion | flops 106170368 | bytes 14292992 | tf_op jit(solution)/shard_map/while/body/eval_jaxpr/gij,gid->gjd/dot_general | solution.py:74
  146.3 7.2 %fusion.164 = bf16[4,128,64]{1,2,0:T(8,128)(2,1)S(1)} fusion(f32[4,128,1536]{2,1,0:T(8,128)} %fusion.160, f32[4,128]{1,0:T(4,128)S(1)} %dynamic-slice_bitcast_fusion.2, bf16[4,1536,256]{1,2,0:T(8,128)(2,1)} %copy-done.2, f32[4,128,1536]{2,1,0:T(8,128)} %get-tuple-element.157, f32[4,128]{1,0:T(4,128)S(1)} %get-tuple-element.158), kind=kOutput, calls=%fused_computation.42.clone.1 | convolution fusion | flops 106203136 | bytes 13441024 | tf_op jit(solution)/shard_map/while/body/eval_jaxpr/gij,gjd->gid/dot_general | solution.py:71
  153.5 8.6 %fusion.161 = f32[4,1536,64]{1,2,0:T(8,128)} fusion(f32[4,128,1536]{2,1,0:T(8,128)} %fusion.160, f32[4,128]{1,0:T(4,128)S(1)} %dynamic-slice_bitcast_fusion.2, bf16[4,128,128]{2,1,0:T(8,128)(2,1)S(1)} %bitcast.111, f32[4,128,1536]{2,1,0:T(8,128)} %get-tuple-element.157, f32[4,128]{1,0:T(4,128)S(1)} %get-tuple-element.158), kind=kOutput, calls=%fused_computation.28.clone.1 | convolution fusion | flops 106170368 | bytes 14292992 | tf_op jit(solution)/shard_map/while/body/eval_jaxpr/gij,gid->gjd/dot_general | solution.py:74
  168.2 6.6 %copy.122 = f32[4,1536,256]{2,1,0:T(8,128)} copy(f32[4,1536,256]{1,2,0:T(8,128)} %pad_maximum_fusion.6) | data formatting | bytes 12582912 | tf_op jit(solution)/shard_map/while/body/eval_jaxpr/concatenate | solution.py:80
  174.8 14.8 %scatter_fusion = f32[32,128,256]{2,1,0:T(8,128)} fusion(f32[32,128,256]{2,1,0:T(8,128)} %get-tuple-element.177, s32[48]{0:T(128)S(1)} %fusion.155, f32[48,128,256]{2,1,0:T(8,128)} %bitcast.96), kind=kCustom, calls=%fused_computation.2.clone.1 | custom fusion | flops 1572864 | bytes 18874560 | tf_op jit(solution)/shard_map/while/body/eval_jaxpr/scatter-add | solution.py:83
  212.2 7.1 %fusion.165 = bf16[4,128,64]{1,2,0:T(8,128)(2,1)S(1)} fusion(f32[4,128,1536]{2,1,0:T(8,128)} %fusion.162, f32[4,128]{1,0:T(4,128)S(1)} %dynamic-slice_bitcast_fusion.2, bf16[4,1536,256]{1,2,0:T(8,128)(2,1)} %copy-done.2, f32[4,128,1536]{2,1,0:T(8,128)} %get-tuple-element.159, f32[4,128]{1,0:T(4,128)S(1)} %get-tuple-element.160), kind=kOutput, calls=%fused_computation.41.clone.1 | convolution fusion | flops 106203136 | bytes 13441024 | tf_op jit(solution)/shard_map/while/body/eval_jaxpr/gij,gjd->gid/dot_general | solution.py:71
  219.3 8.5 %fusion.163 = f32[4,1536,64]{1,2,0:T(8,128)} fusion(f32[4,128,1536]{2,1,0:T(8,128)} %fusion.162, f32[4,128]{1,0:T(4,128)S(1)} %dynamic-slice_bitcast_fusion.2, bf16[4,128,128]{2,1,0:T(8,128)(2,1)S(1)} %bitcast.109, f32[4,128,1536]{2,1,0:T(8,128)} %get-tuple-element.159, f32[4,128]{1,0:T(4,128)S(1)} %get-tuple-element.160), kind=kOutput, calls=%fused_computation.30.clone.1 | convolution fusion | flops 106170368 | bytes 14292992 | tf_op jit(solution)/shard_map/while/body/eval_jaxpr/gij,gid->gjd/dot_general | solution.py:74
  235.0 7.2 %fusion.164 = bf16[4,128,64]{1,2,0:T(8,128)(2,1)S(1)} fusion(f32[4,128,1536]{2,1,0:T(8,128)} %fusion.160, f32[4,128]{1,0:T(4,128)S(1)} %dynamic-slice_bitcast_fusion.2, bf16[4,1536,256]{1,2,0:T(8,128)(2,1)} %copy-done.2, f32[4,128,1536]{2,1,0:T(8,128)} %get-tuple-element.157, f32[4,128]{1,0:T(4,128)S(1)} %get-tuple-element.158), kind=kOutput, calls=%fused_computation.42.clone.1 | convolution fusion | flops 106203136 | bytes 13441024 | tf_op jit(solution)/shard_map/while/body/eval_jaxpr/gij,gjd->gid/dot_general | solution.py:71
  242.2 8.6 %fusion.161 = f32[4,1536,64]{1,2,0:T(8,128)} fusion(f32[4,128,1536]{2,1,0:T(8,128)} %fusion.160, f32[4,128]{1,0:T(4,128)S(1)} %dynamic-slice_bitcast_fusion.2, bf16[4,128,128]{2,1,0:T(8,128)(2,1)S(1)} %bitcast.111, f32[4,128,1536]{2,1,0:T(8,128)} %get-tuple-element.157, f32[4,128]{1,0:T(4,128)S(1)} %get-tuple-element.158), kind=kOutput, calls=%fused_computation.28.clone.1 | convolution fusion | flops 106170368 | bytes 14292992 | tf_op jit(solution)/shard_map/while/body/eval_jaxpr/gij,gid->gjd/dot_general | solution.py:74
  256.9 6.6 %copy.122 = f32[4,1536,256]{2,1,0:T(8,128)} copy(f32[4,1536,256]{1,2,0:T(8,128)} %pad_maximum_fusion.6) | data formatting | bytes 12582912 | tf_op jit(solution)/shard_map/while/body/eval_jaxpr/concatenate | solution.py:80
  263.5 14.7 %scatter_fusion = f32[32,128,256]{2,1,0:T(8,128)} fusion(f32[32,128,256]{2,1,0:T(8,128)} %get-tuple-element.177, s32[48]{0:T(128)S(1)} %fusion.155, f32[48,128,256]{2,1,0:T(8,128)} %bitcast.96), kind=kCustom, calls=%fused_computation.2.clone.1 | custom fusion | flops 1572864 | bytes 18874560 | tf_op jit(solution)/shard_map/while/body/eval_jaxpr/scatter-add | solution.py:83
  300.8 7.1 %fusion.165 = bf16[4,128,64]{1,2,0:T(8,128)(2,1)S(1)} fusion(f32[4,128,1536]{2,1,0:T(8,128)} %fusion.162, f32[4,128]{1,0:T(4,128)S(1)} %dynamic-slice_bitcast_fusion.2, bf16[4,1536,256]{1,2,0:T(8,128)(2,1)} %copy-done.2, f32[4,128,1536]{2,1,0:T(8,128)} %get-tuple-element.159, f32[4,128]{1,0:T(4,128)S(1)} %get-tuple-element.160), kind=kOutput, calls=%fused_computation.41.clone.1 | convolution fusion | flops 106203136 | bytes 13441024 | tf_op jit(solution)/shard_map/while/body/eval_jaxpr/gij,gjd->gid/dot_general | solution.py:71
  307.9 8.5 %fusion.163 = f32[4,1536,64]{1,2,0:T(8,128)} fusion(f32[4,128,1536]{2,1,0:T(8,128)} %fusion.162, f32[4,128]{1,0:T(4,128)S(1)} %dynamic-slice_bitcast_fusion.2, bf16[4,128,128]{2,1,0:T(8,128)(2,1)S(1)} %bitcast.109, f32[4,128,1536]{2,1,0:T(8,128)} %get-tuple-element.159, f32[4,128]{1,0:T(4,128)S(1)} %get-tuple-element.160), kind=kOutput, calls=%fused_computation.30.clone.1 | convolution fusion | flops 106170368 | bytes 14292992 | tf_op jit(solution)/shard_map/while/body/eval_jaxpr/gij,gid->gjd/dot_general | solution.py:74
  323.6 7.2 %fusion.164 = bf16[4,128,64]{1,2,0:T(8,128)(2,1)S(1)} fusion(f32[4,128,1536]{2,1,0:T(8,128)} %fusion.160, f32[4,128]{1,0:T(4,128)S(1)} %dynamic-slice_bitcast_fusion.2, bf16[4,1536,256]{1,2,0:T(8,128)(2,1)} %copy-done.2, f32[4,128,1536]{2,1,0:T(8,128)} %get-tuple-element.157, f32[4,128]{1,0:T(4,128)S(1)} %get-tuple-element.158), kind=kOutput, calls=%fused_computation.42.clone.1 | convolution fusion | flops 106203136 | bytes 13441024 | tf_op jit(solution)/shard_map/while/body/eval_jaxpr/gij,gjd->gid/dot_general | solution.py:71
  330.8 8.6 %fusion.161 = f32[4,1536,64]{1,2,0:T(8,128)} fusion(f32[4,128,1536]{2,1,0:T(8,128)} %fusion.160, f32[4,128]{1,0:T(4,128)S(1)} %dynamic-slice_bitcast_fusion.2, bf16[4,128,128]{2,1,0:T(8,128)(2,1)S(1)} %bitcast.111, f32[4,128,1536]{2,1,0:T(8,128)} %get-tuple-element.157, f32[4,128]{1,0:T(4,128)S(1)} %get-tuple-element.158), kind=kOutput, calls=%fused_computation.28.clone.1 | convolution fusion | flops 106170368 | bytes 14292992 | tf_op jit(solution)/shard_map/while/body/eval_jaxpr/gij,gid->gjd/dot_general | solution.py:74
  352.1 14.8 %scatter_fusion = f32[32,128,256]{2,1,0:T(8,128)} fusion(f32[32,128,256]{2,1,0:T(8,128)} %get-tuple-element.177, s32[48]{0:T(128)S(1)} %fusion.155, f32[48,128,256]{2,1,0:T(8,128)} %bitcast.96), kind=kCustom, calls=%fused_computation.2.clone.1 | custom fusion | flops 1572864 | bytes 18874560 | tf_op jit(solution)/shard_map/while/body/eval_jaxpr/scatter-add | solution.py:83
  389.5 7.1 %fusion.165 = bf16[4,128,64]{1,2,0:T(8,128)(2,1)S(1)} fusion(f32[4,128,1536]{2,1,0:T(8,128)} %fusion.162, f32[4,128]{1,0:T(4,128)S(1)} %dynamic-slice_bitcast_fusion.2, bf16[4,1536,256]{1,2,0:T(8,128)(2,1)} %copy-done.2, f32[4,128,1536]{2,1,0:T(8,128)} %get-tuple-element.159, f32[4,128]{1,0:T(4,128)S(1)} %get-tuple-element.160), kind=kOutput, calls=%fused_computation.41.clone.1 | convolution fusion | flops 106203136 | bytes 13441024 | tf_op jit(solution)/shard_map/while/body/eval_jaxpr/gij,gjd->gid/dot_general | solution.py:71
  396.6 8.5 %fusion.163 = f32[4,1536,64]{1,2,0:T(8,128)} fusion(f32[4,128,1536]{2,1,0:T(8,128)} %fusion.162, f32[4,128]{1,0:T(4,128)S(1)} %dynamic-slice_bitcast_fusion.2, bf16[4,128,128]{2,1,0:T(8,128)(2,1)S(1)} %bitcast.109, f32[4,128,1536]{2,1,0:T(8,128)} %get-tuple-element.159, f32[4,128]{1,0:T(4,128)S(1)} %get-tuple-element.160), kind=kOutput, calls=%fused_computation.30.clone.1 | convolution fusion | flops 106170368 | bytes 14292992 | tf_op jit(solution)/shard_map/while/body/eval_jaxpr/gij,gid->gjd/dot_general | solution.py:74
  412.4 7.2 %fusion.164 = bf16[4,128,64]{1,2,0:T(8,128)(2,1)S(1)} fusion(f32[4,128,1536]{2,1,0:T(8,128)} %fusion.160, f32[4,128]{1,0:T(4,128)S(1)} %dynamic-slice_bitcast_fusion.2, bf16[4,1536,256]{1,2,0:T(8,128)(2,1)} %copy-done.2, f32[4,128,1536]{2,1,0:T(8,128)} %get-tuple-element.157, f32[4,128]{1,0:T(4,128)S(1)} %get-tuple-element.158), kind=kOutput, calls=%fused_computation.42.clone.1 | convolution fusion | flops 106203136 | bytes 13441024 | tf_op jit(solution)/shard_map/while/body/eval_jaxpr/gij,gjd->gid/dot_general | solution.py:71
  419.5 8.6 %fusion.161 = f32[4,1536,64]{1,2,0:T(8,128)} fusion(f32[4,128,1536]{2,1,0:T(8,128)} %fusion.160, f32[4,128]{1,0:T(4,128)S(1)} %dynamic-slice_bitcast_fusion.2, bf16[4,128,128]{2,1,0:T(8,128)(2,1)S(1)} %bitcast.111, f32[4,128,1536]{2,1,0:T(8,128)} %get-tuple-element.157, f32[4,128]{1,0:T(4,128)S(1)} %get-tuple-element.158), kind=kOutput, calls=%fused_computation.28.clone.1 | convolution fusion | flops 106170368 | bytes 14292992 | tf_op jit(solution)/shard_map/while/body/eval_jaxpr/gij,gid->gjd/dot_general | solution.py:74
  440.9 14.8 %scatter_fusion = f32[32,128,256]{2,1,0:T(8,128)} fusion(f32[32,128,256]{2,1,0:T(8,128)} %get-tuple-element.177, s32[48]{0:T(128)S(1)} %fusion.155, f32[48,128,256]{2,1,0:T(8,128)} %bitcast.96), kind=kCustom, calls=%fused_computation.2.clone.1 | custom fusion | flops 1572864 | bytes 18874560 | tf_op jit(solution)/shard_map/while/body/eval_jaxpr/scatter-add | solution.py:83
  458.2 16.6 %all_to_all.137 = bf16[16,128,256]{2,1,0:T(8,128)(2,1)S(1)} all-to-all(bf16[16,128,256]{2,1,0:T(8,128)(2,1)S(1)} %slice.107), channel_id=1, replica_groups=mesh['dom'=4,'head'=8] {'dom'}, dimensions={0} | all-to-all | bytes 2097152 | tf_op jit(solution)/shard_map/all_to_all | solution.py:90
  484.9 8.8 %all-to-all-done.5 = bf16[8,256,128]{2,1,0:T(8,128)(2,1)S(1)} async-done(((bf16[8,256,128]{2,1,0:T(8,128)(2,1)}), bf16[8,256,128]{2,1,0:T(8,128)(2,1)S(1)}, u32[]{:S(2)}, u32[]{:S(2)}) %all-to-all-start.5) | async-done | bytes 524320 | tf_op jit(solution)/shard_map/all_to_all | solution.py:100
  498.1 14.3 %all-to-all-done.8 = bf16[8,256,128]{2,1,0:T(8,128)(2,1)S(1)} async-done(((bf16[8,256,128]{2,1,0:T(8,128)(2,1)}), bf16[8,256,128]{2,1,0:T(8,128)(2,1)S(1)}, u32[]{:S(2)}, u32[]{:S(2)}) %all-to-all-start.8) | async-done | bytes 524320 | tf_op jit(solution)/shard_map/all_to_all | solution.py:102
  518.4 12.8 %all-to-all-done.7 = bf16[8,256,128]{2,1,0:T(8,128)(2,1)S(1)} async-done(((bf16[8,256,128]{2,1,0:T(8,128)(2,1)}), bf16[8,256,128]{2,1,0:T(8,128)(2,1)S(1)}, u32[]{:S(2)}, u32[]{:S(2)}) %all-to-all-start.7) | async-done | bytes 524320 | tf_op jit(solution)/shard_map/all_to_all | solution.py:101
  (174 shorter events, 209.5 us)
Async XLA Ops:
  0.6 1.1 copy-start
  0.6 27.1 %copy-start.7 = (bf16[256,1024]{1,0:T(8,128)(2,1)S(1)}, bf16[256,1024]{1,0:T(8,128)(2,1)}, u32[]{:S(2)}) copy-start(bf16[256,1024]{1,0:T(8,128)(2,1)} %param.9) | copy-start | bytes 1572868
  2.6 21.7 %all-to-all-start.1 = ((bf16[256,8,128]{2,0,1:T(8,128)(2,1)}), bf16[256,8,128]{2,0,1:T(8,128)(2,1)S(1)}, u32[]{:S(2)}, u32[]{:S(2)}) async-start(bf16[256,8,128]{2,0,1:T(8,128)(2,1)} %copy_bitcast_fusion.3), calls=%async_computation.1 | async-start | bytes 1048576 | tf_op jit(solution)/shard_map/all_to_all | solution.py:30
  24.3 18.8 %all-to-all-start.2 = ((bf16[256,8,128]{2,0,1:T(8,128)(2,1)}), bf16[256,8,128]{2,0,1:T(8,128)(2,1)S(1)}, u32[]{:S(2)}, u32[]{:S(2)}) async-start(bf16[256,8,128]{2,0,1:T(8,128)(2,1)} %copy_bitcast_fusion.2), calls=%async_computation.2 | async-start | bytes 1048576 | tf_op jit(solution)/shard_map/all_to_all | solution.py:31
  43.0 19.5 %all-to-all-start = ((bf16[256,8,128]{2,0,1:T(8,128)(2,1)}), bf16[256,8,128]{2,0,1:T(8,128)(2,1)}, u32[]{:S(2)}, u32[]{:S(2)}) async-start(bf16[256,8,128]{2,0,1:T(8,128)(2,1)} %copy_bitcast_fusion.4), calls=%async_computation | async-start | bytes 1048576 | tf_op jit(solution)/shard_map/all_to_all | solution.py:29
  48.0 0.5 copy-start.10
  49.2 17.1 %copy-start.8 = (bf16[256,1024]{1,0:T(8,128)(2,1)S(1)}, bf16[256,1024]{1,0:T(8,128)(2,1)}, u32[]{:S(2)}) copy-start(bf16[256,1024]{1,0:T(8,128)(2,1)} %param.12) | copy-start | bytes 1572868
  49.2 34.7 %copy-start.9 = (s32[2048]{0:T(1024)S(1)}, s32[2048]{0:T(1024)}, u32[]{:S(2)}) copy-start(s32[2048]{0:T(1024)} %param.13) | copy-start | bytes 24580
  62.5 17.2 %all-to-all-start.3 = ((bf16[16,128,256]{2,1,0:T(8,128)(2,1)}), bf16[16,128,256]{2,1,0:T(8,128)(2,1)S(1)}, u32[]{:S(2)}, u32[]{:S(2)}) async-start(bf16[16,128,256]{2,1,0:T(8,128)(2,1)} %broadcast_select_fusion.1), calls=%async_computation.3 | async-start | bytes 2097152 | tf_op jit(solution)/shard_map/all_to_all | solution.py:18
  79.7 4.2 copy-start.6
  79.8 19.5 %all-to-all-start.4 = ((bf16[256,8,128]{2,0,1:T(8,128)(2,1)}), bf16[256,8,128]{2,0,1:T(8,128)(2,1)}, u32[]{:S(2)}, u32[]{:S(2)}) async-start(bf16[256,8,128]{2,0,1:T(8,128)(2,1)} %copy_bitcast_fusion.1), calls=%async_computation.4 | async-start | bytes 1048576 | tf_op jit(solution)/shard_map/all_to_all | solution.py:32
  114.9 2.6 copy-start.2
  162.1 2.6 copy-start.3
  162.1 2.8 copy-start.4
  162.1 3.3 copy-start.5
  203.6 2.6 copy-start.2
  250.8 2.6 copy-start.3
  250.8 2.8 copy-start.4
  250.8 3.3 copy-start.5
  292.2 2.6 copy-start.2
  339.4 2.6 copy-start.3
  339.4 2.8 copy-start.4
  339.4 3.3 copy-start.5
  380.9 2.6 copy-start.2
  428.1 2.6 copy-start.3
  428.1 2.8 copy-start.4
  428.1 3.3 copy-start.5
  474.9 18.8 %all-to-all-start.5 = ((bf16[8,256,128]{2,1,0:T(8,128)(2,1)}), bf16[8,256,128]{2,1,0:T(8,128)(2,1)S(1)}, u32[]{:S(2)}, u32[]{:S(2)}) async-start(bf16[8,256,128]{2,1,0:T(8,128)(2,1)} %bitcast.17), calls=%async_computation.5 | async-start | bytes 1048576 | tf_op jit(solution)/shard_map/all_to_all | solution.py:100
  478.4 4.6 copy-start.11
  493.6 18.8 %all-to-all-start.8 = ((bf16[8,256,128]{2,1,0:T(8,128)(2,1)}), bf16[8,256,128]{2,1,0:T(8,128)(2,1)S(1)}, u32[]{:S(2)}, u32[]{:S(2)}) async-start(bf16[8,256,128]{2,1,0:T(8,128)(2,1)} %bitcast.25), calls=%async_computation.8 | async-start | bytes 1048576 | tf_op jit(solution)/shard_map/all_to_all | solution.py:102
  512.4 18.8 %all-to-all-start.7 = ((bf16[8,256,128]{2,1,0:T(8,128)(2,1)}), bf16[8,256,128]{2,1,0:T(8,128)(2,1)S(1)}, u32[]{:S(2)}, u32[]{:S(2)}) async-start(bf16[8,256,128]{2,1,0:T(8,128)(2,1)} %bitcast.22), calls=%async_computation.7 | async-start | bytes 1048576 | tf_op jit(solution)/shard_map/all_to_all | solution.py:101
  515.9 16.5 %copy-start.1 = (bf16[256,1024]{1,0:T(8,128)(2,1)S(1)}, bf16[256,1024]{1,0:T(8,128)(2,1)}, u32[]{:S(2)}) copy-start(bf16[256,1024]{1,0:T(8,128)(2,1)} %param.10) | copy-start | bytes 1572868
where the time goes:
time: 535 us; the launch traced here: 532 us
  matrix products  200 us (37%)
  waiting for transfers between devices  102 us (19%)
  local copies, waits for them, and re-layouts  89.5 us (17%)
  other arithmetic  85.4 us (16%)
  starting transfers between devices  32.3 us (6%)
  blocking collectives  16.6 us (3%)
  loops' own time  5.52 us (1%)
    dot_general x8, matrix products, group(): jnp.einsum('gij,gid->gjd', dscores, query_one, preferred_element_type=jnp...  68.3 us
    scatter-add x4, other arithmetic, group(): acc = acc.at[picks].add(contrib)  59 us
    dot_general x8, matrix products, group(): jnp.einsum('gij,gjd->gid', dscores, keys_n, preferred_element_type=jnp.fl...  57 us
    sub x8, matrix products, group(): expo = jnp.exp(scores - top)  29.9 us
    gather x8, local copies, waits for them, and re-layouts, group(): gathered = jnp.take(table, picks, axis=0).reshape(4, span, 2 * width)  28.6 us
    concatenate x4, local copies, waits for them, and re-layouts, group(): jnp.concatenate(grad_k_heads + grad_v_heads, -1)  26.3 us
    dot_general x8, matrix products, group(): jnp.einsum('gij,gid->gjd', probs_b, grad_one, preferred_element_type=jnp....  24.4 us
    dot_general x8, matrix products, group(): jnp.einsum('gid,gjd->gij', grad_one, values_n, preferred_element_type=jnp...  19.4 us
  transfers between devices with their start and end apart: 8, of which 8 were waited for; matrix products, arithmetic and copies ran while one was open for 3% of the time, Pallas kernels for 0%

commit v1 on v0

--- a/solution.py
+++ b/solution.py
@@ -8,6 +8,29 @@
 H = 16
 NBR = 12
 BS = 128
+
+
+def split_up(value, dim, devices):
+    dims = value.shape
+    blocks = value.reshape(*dims[:dim], devices, dims[dim] // devices, *dims[dim + 1 :])
+    return jnp.moveaxis(blocks, dim, 0)
+
+
+def in_order(blocks, dim):
+    shape = list(blocks.shape[1:])
+    shape[dim] *= blocks.shape[0]
+    return jnp.moveaxis(blocks, 0, dim).reshape(shape)
+
+
+def swapped_with_each(shard, axis, split_dim, concat_dim):
+    length, mine = (lax.axis_size(axis), lax.axis_index(axis))
+    parts = split_up(shard, split_dim, length)
+    outs = [parts[mine]]
+    for step in range(1, length):
+        sent = parts[mine ^ step]
+        outs.append(lax.ppermute(sent, axis, [(i, i ^ step) for i in range(length)]))
+    parts = jnp.stack(outs)[mine ^ jnp.arange(length)]
+    return in_order(parts, concat_dim)
 
 
 def borrow_table(keys_h, values_h, my_lists, block):
@@ -29,7 +52,7 @@
         lax.all_to_all(node_queries, "head", split_axis=1, concat_axis=0, tiled=True),
         lax.all_to_all(node_keys, "head", split_axis=1, concat_axis=0, tiled=True),
         lax.all_to_all(node_values, "head", split_axis=1, concat_axis=0, tiled=True),
-        lax.all_to_all(out_grad, "head", split_axis=1, concat_axis=0, tiled=True),
+        swapped_with_each(out_grad, "head", 1, 0),
     )
     table = borrow_table(keys_h, values_h, my_lists, block)
     rows, width = queries.shape

time: 535 us -> 519 us (0.970)
  waiting for transfers between devices: 102 us -> 73.6 us
  local copies, waits for them, and re-layouts: 89.5 us -> 95.9 us
    all_to_all x1 -> x0, waiting for transfers between devices: 13.9 us -> none  [body(): lax.all_to_all(out_grad, 'head', split_axis=1, concat_axis=0, tiled=True)]
    all_to_all x1, waiting for transfers between devices: 13.4 us -> 3.15 us  [body(): lax.all_to_all(node_keys, 'head', split_axis=1, concat_axis=0, tiled=True)]
    ppermute x0 -> x7, starting transfers between devices: none -> 7.82 us  [swapped_with_each(): lax.ppermute(sent, axis, [(i, i ^ step) for i in range(length)])]
  transfers between devices with their start and end apart: 8 -> 14, of which waited for: 8 -> 7; matrix products, arithmetic and copies ran while one was open for 3% -> 5% of each run, Pallas kernels for 0% -> 0%
where the time goes in v1:
time: 519 us; the launch traced here: 517 us
  matrix products  200 us (39%)
  local copies, waits for them, and re-layouts  95.9 us (18%)
  other arithmetic  87.3 us (17%)
  waiting for transfers between devices  73.6 us (14%)
  starting transfers between devices  36.1 us (7%)
  blocking collectives  16.7 us (3%)
  loops' own time  5.52 us (1%)
    dot_general x8, matrix products, group(): jnp.einsum('gij,gid->gjd', dscores, query_one, preferred_element_type=jnp...  68.7 us
    scatter-add x4, other arithmetic, group(): acc = acc.at[picks].add(contrib)  59.2 us
    dot_general x8, matrix products, group(): jnp.einsum('gij,gjd->gid', dscores, keys_n, preferred_element_type=jnp.fl...  57.3 us
    sub x8, matrix products, group(): expo = jnp.exp(scores - top)  29.9 us
    gather x8, local copies, waits for them, and re-layouts, group(): gathered = jnp.take(table, picks, axis=0).reshape(4, span, 2 * width)  28.7 us
    concatenate x4, local copies, waits for them, and re-layouts, group(): jnp.concatenate(grad_k_heads + grad_v_heads, -1)  26.4 us
    dot_general x8, matrix products, group(): jnp.einsum('gij,gid->gjd', probs_b, grad_one, preferred_element_type=jnp....  24.3 us
    dot_general x8, matrix products, group(): jnp.einsum('gid,gjd->gij', grad_one, values_n, preferred_element_type=jnp...  19.4 us
  transfers between devices with their start and end apart: 14, of which 7 were waited for; matrix products, arithmetic and copies ran while one was open for 5% of the time, Pallas kernels for 0%

profile of v1, /device:TPU:0, one launch (start us, length us, event | category | flops | bytes accessed | tf_op | source)
XLA Modules:
  0.0 516.6 jit_solution(14559993226707248072)
XLA Ops:
  30.5 13.1 %all-to-all-done.2 = bf16[256,8,128]{2,0,1:T(8,128)(2,1)S(1)} async-done(((bf16[256,8,128]{2,0,1:T(8,128)(2,1)}), bf16[256,8,128]{2,0,1:T(8,128)(2,1)S(1)}, u32[]{:S(2)}, u32[]{:S(2)}) %all-to-all-start.2) | async-done | bytes 524320 | tf_op jit(solution)/shard_map/all_to_all | solution.py:54
  54.0 9.0 %all-to-all-done.3 = bf16[16,128,256]{2,1,0:T(8,128)(2,1)S(1)} async-done(((bf16[16,128,256]{2,1,0:T(8,128)(2,1)}), bf16[16,128,256]{2,1,0:T(8,128)(2,1)S(1)}, u32[]{:S(2)}, u32[]{:S(2)}) %all-to-all-start.3) | async-done | bytes 1048608 | tf_op jit(solution)/shard_map/all_to_all | solution.py:41
  70.1 12.4 %all-to-all-done = bf16[256,8,128]{2,0,1:T(8,128)(2,1)} async-done(((bf16[256,8,128]{2,0,1:T(8,128)(2,1)}), bf16[256,8,128]{2,0,1:T(8,128)(2,1)}, u32[]{:S(2)}, u32[]{:S(2)}) %all-to-all-start) | async-done | bytes 524320 | tf_op jit(solution)/shard_map/all_to_all | solution.py:52
  84.9 355.7 %while.12 = (s32[]{:T(128)}, f32[32,128,256]{2,1,0:T(8,128)}, bf16[4,512,128]{2,1,0:T(8,128)(2,1)}, s32[4]{0:T(128)S(1)}, s32[16,12]{1,0:T(8,128)}, /*index=5*/b...) while((s32[]{:T(128)}, f32[32,128,256]{2,1,0:T(8,128)}, ...), condition=%wide.region_8.9_spmd, body=%wide.region_0.8_spmd.sunk | while | flops 1044722112 | bytes 177150128 | solution.py:110
  106.7 7.1 %fusion.166 = bf16[4,128,64]{1,2,0:T(8,128)(2,1)S(1)} fusion(f32[4,128,1536]{2,1,0:T(8,128)} %fusion.163, f32[4,128]{1,0:T(4,128)S(1)} %dynamic-slice_bitcast_fusion.2, bf16[4,1536,256]{1,2,0:T(8,128)(2,1)} %copy-done.2, f32[4,128,1536]{2,1,0:T(8,128)} %get-tuple-element.167, f32[4,128]{1,0:T(4,128)S(1)} %get-tuple-element.168), kind=kOutput, calls=%fused_computation.42.clone.1 | convolution fusion | flops 106203136 | bytes 13441024 | tf_op jit(solution)/shard_map/while/body/eval_jaxpr/gij,gjd->gid/dot_general | solution.py:94
  113.8 8.5 %fusion.164 = f32[4,1536,64]{1,2,0:T(8,128)} fusion(f32[4,128,1536]{2,1,0:T(8,128)} %fusion.163, f32[4,128]{1,0:T(4,128)S(1)} %dynamic-slice_bitcast_fusion.2, bf16[4,128,128]{2,1,0:T(8,128)(2,1)S(1)} %bitcast.128, f32[4,128,1536]{2,1,0:T(8,128)} %get-tuple-element.167, f32[4,128]{1,0:T(4,128)S(1)} %get-tuple-element.168), kind=kOutput, calls=%fused_computation.31.clone.1 | convolution fusion | flops 106170368 | bytes 14292992 | tf_op jit(solution)/shard_map/while/body/eval_jaxpr/gij,gid->gjd/dot_general | solution.py:97
  129.5 7.2 %fusion.165 = bf16[4,128,64]{1,2,0:T(8,128)(2,1)S(1)} fusion(f32[4,128,1536]{2,1,0:T(8,128)} %fusion.161, f32[4,128]{1,0:T(4,128)S(1)} %dynamic-slice_bitcast_fusion.2, bf16[4,1536,256]{1,2,0:T(8,128)(2,1)} %copy-done.2, f32[4,128,1536]{2,1,0:T(8,128)} %get-tuple-element.165, f32[4,128]{1,0:T(4,128)S(1)} %get-tuple-element.166), kind=kOutput, calls=%fused_computation.43.clone.1 | convolution fusion | flops 106203136 | bytes 13441024 | tf_op jit(solution)/shard_map/while/body/eval_jaxpr/gij,gjd->gid/dot_general | solution.py:94
  136.8 8.7 %fusion.162 = f32[4,1536,64]{1,2,0:T(8,128)} fusion(f32[4,128,1536]{2,1,0:T(8,128)} %fusion.161, f32[4,128]{1,0:T(4,128)S(1)} %dynamic-slice_bitcast_fusion.2, bf16[4,128,128]{2,1,0:T(8,128)(2,1)S(1)} %bitcast.130, f32[4,128,1536]{2,1,0:T(8,128)} %get-tuple-element.165, f32[4,128]{1,0:T(4,128)S(1)} %get-tuple-element.166), kind=kOutput, calls=%fused_computation.29.clone.1 | convolution fusion | flops 106170368 | bytes 14292992 | tf_op jit(solution)/shard_map/while/body/eval_jaxpr/gij,gid->gjd/dot_general | solution.py:97
  151.6 6.6 %copy.142 = f32[4,1536,256]{2,1,0:T(8,128)} copy(f32[4,1536,256]{1,2,0:T(8,128)} %pad_maximum_fusion.6) | data formatting | bytes 12582912 | tf_op jit(solution)/shard_map/while/body/eval_jaxpr/concatenate | solution.py:103
  158.2 14.9 %scatter_fusion = f32[32,128,256]{2,1,0:T(8,128)} fusion(f32[32,128,256]{2,1,0:T(8,128)} %get-tuple-element.185, s32[48]{0:T(128)S(1)} %fusion.156, f32[48,128,256]{2,1,0:T(8,128)} %bitcast.115), kind=kCustom, calls=%fused_computation.3.clone.1 | custom fusion | flops 1572864 | bytes 18874560 | tf_op jit(solution)/shard_map/while/body/eval_jaxpr/scatter-add | solution.py:106
  195.7 7.1 %fusion.166 = bf16[4,128,64]{1,2,0:T(8,128)(2,1)S(1)} fusion(f32[4,128,1536]{2,1,0:T(8,128)} %fusion.163, f32[4,128]{1,0:T(4,128)S(1)} %dynamic-slice_bitcast_fusion.2, bf16[4,1536,256]{1,2,0:T(8,128)(2,1)} %copy-done.2, f32[4,128,1536]{2,1,0:T(8,128)} %get-tuple-element.167, f32[4,128]{1,0:T(4,128)S(1)} %get-tuple-element.168), kind=kOutput, calls=%fused_computation.42.clone.1 | convolution fusion | flops 106203136 | bytes 13441024 | tf_op jit(solution)/shard_map/while/body/eval_jaxpr/gij,gjd->gid/dot_general | solution.py:94
  202.8 8.5 %fusion.164 = f32[4,1536,64]{1,2,0:T(8,128)} fusion(f32[4,128,1536]{2,1,0:T(8,128)} %fusion.163, f32[4,128]{1,0:T(4,128)S(1)} %dynamic-slice_bitcast_fusion.2, bf16[4,128,128]{2,1,0:T(8,128)(2,1)S(1)} %bitcast.128, f32[4,128,1536]{2,1,0:T(8,128)} %get-tuple-element.167, f32[4,128]{1,0:T(4,128)S(1)} %get-tuple-element.168), kind=kOutput, calls=%fused_computation.31.clone.1 | convolution fusion | flops 106170368 | bytes 14292992 | tf_op jit(solution)/shard_map/while/body/eval_jaxpr/gij,gid->gjd/dot_general | solution.py:97
  218.5 7.2 %fusion.165 = bf16[4,128,64]{1,2,0:T(8,128)(2,1)S(1)} fusion(f32[4,128,1536]{2,1,0:T(8,128)} %fusion.161, f32[4,128]{1,0:T(4,128)S(1)} %dynamic-slice_bitcast_fusion.2, bf16[4,1536,256]{1,2,0:T(8,128)(2,1)} %copy-done.2, f32[4,128,1536]{2,1,0:T(8,128)} %get-tuple-element.165, f32[4,128]{1,0:T(4,128)S(1)} %get-tuple-element.166), kind=kOutput, calls=%fused_computation.43.clone.1 | convolution fusion | flops 106203136 | bytes 13441024 | tf_op jit(solution)/shard_map/while/body/eval_jaxpr/gij,gjd->gid/dot_general | solution.py:94
  225.8 8.7 %fusion.162 = f32[4,1536,64]{1,2,0:T(8,128)} fusion(f32[4,128,1536]{2,1,0:T(8,128)} %fusion.161, f32[4,128]{1,0:T(4,128)S(1)} %dynamic-slice_bitcast_fusion.2, bf16[4,128,128]{2,1,0:T(8,128)(2,1)S(1)} %bitcast.130, f32[4,128,1536]{2,1,0:T(8,128)} %get-tuple-element.165, f32[4,128]{1,0:T(4,128)S(1)} %get-tuple-element.166), kind=kOutput, calls=%fused_computation.29.clone.1 | convolution fusion | flops 106170368 | bytes 14292992 | tf_op jit(solution)/shard_map/while/body/eval_jaxpr/gij,gid->gjd/dot_general | solution.py:97
  240.6 6.6 %copy.142 = f32[4,1536,256]{2,1,0:T(8,128)} copy(f32[4,1536,256]{1,2,0:T(8,128)} %pad_maximum_fusion.6) | data formatting | bytes 12582912 | tf_op jit(solution)/shard_map/while/body/eval_jaxpr/concatenate | solution.py:103
  247.2 14.7 %scatter_fusion = f32[32,128,256]{2,1,0:T(8,128)} fusion(f32[32,128,256]{2,1,0:T(8,128)} %get-tuple-element.185, s32[48]{0:T(128)S(1)} %fusion.156, f32[48,128,256]{2,1,0:T(8,128)} %bitcast.115), kind=kCustom, calls=%fused_computation.3.clone.1 | custom fusion | flops 1572864 | bytes 18874560 | tf_op jit(solution)/shard_map/while/body/eval_jaxpr/scatter-add | solution.py:106
  284.5 7.1 %fusion.166 = bf16[4,128,64]{1,2,0:T(8,128)(2,1)S(1)} fusion(f32[4,128,1536]{2,1,0:T(8,128)} %fusion.163, f32[4,128]{1,0:T(4,128)S(1)} %dynamic-slice_bitcast_fusion.2, bf16[4,1536,256]{1,2,0:T(8,128)(2,1)} %copy-done.2, f32[4,128,1536]{2,1,0:T(8,128)} %get-tuple-element.167, f32[4,128]{1,0:T(4,128)S(1)} %get-tuple-element.168), kind=kOutput, calls=%fused_computation.42.clone.1 | convolution fusion | flops 106203136 | bytes 13441024 | tf_op jit(solution)/shard_map/while/body/eval_jaxpr/gij,gjd->gid/dot_general | solution.py:94
  291.6 8.5 %fusion.164 = f32[4,1536,64]{1,2,0:T(8,128)} fusion(f32[4,128,1536]{2,1,0:T(8,128)} %fusion.163, f32[4,128]{1,0:T(4,128)S(1)} %dynamic-slice_bitcast_fusion.2, bf16[4,128,128]{2,1,0:T(8,128)(2,1)S(1)} %bitcast.128, f32[4,128,1536]{2,1,0:T(8,128)} %get-tuple-element.167, f32[4,128]{1,0:T(4,128)S(1)} %get-tuple-element.168), kind=kOutput, calls=%fused_computation.31.clone.1 | convolution fusion | flops 106170368 | bytes 14292992 | tf_op jit(solution)/shard_map/while/body/eval_jaxpr/gij,gid->gjd/dot_general | solution.py:97
  307.4 7.2 %fusion.165 = bf16[4,128,64]{1,2,0:T(8,128)(2,1)S(1)} fusion(f32[4,128,1536]{2,1,0:T(8,128)} %fusion.161, f32[4,128]{1,0:T(4,128)S(1)} %dynamic-slice_bitcast_fusion.2, bf16[4,1536,256]{1,2,0:T(8,128)(2,1)} %copy-done.2, f32[4,128,1536]{2,1,0:T(8,128)} %get-tuple-element.165, f32[4,128]{1,0:T(4,128)S(1)} %get-tuple-element.166), kind=kOutput, calls=%fused_computation.43.clone.1 | convolution fusion | flops 106203136 | bytes 13441024 | tf_op jit(solution)/shard_map/while/body/eval_jaxpr/gij,gjd->gid/dot_general | solution.py:94
  314.6 8.7 %fusion.162 = f32[4,1536,64]{1,2,0:T(8,128)} fusion(f32[4,128,1536]{2,1,0:T(8,128)} %fusion.161, f32[4,128]{1,0:T(4,128)S(1)} %dynamic-slice_bitcast_fusion.2, bf16[4,128,128]{2,1,0:T(8,128)(2,1)S(1)} %bitcast.130, f32[4,128,1536]{2,1,0:T(8,128)} %get-tuple-element.165, f32[4,128]{1,0:T(4,128)S(1)} %get-tuple-element.166), kind=kOutput, calls=%fused_computation.29.clone.1 | convolution fusion | flops 106170368 | bytes 14292992 | tf_op jit(solution)/shard_map/while/body/eval_jaxpr/gij,gid->gjd/dot_general | solution.py:97
  329.4 6.6 %copy.142 = f32[4,1536,256]{2,1,0:T(8,128)} copy(f32[4,1536,256]{1,2,0:T(8,128)} %pad_maximum_fusion.6) | data formatting | bytes 12582912 | tf_op jit(solution)/shard_map/while/body/eval_jaxpr/concatenate | solution.py:103
  336.0 14.8 %scatter_fusion = f32[32,128,256]{2,1,0:T(8,128)} fusion(f32[32,128,256]{2,1,0:T(8,128)} %get-tuple-element.185, s32[48]{0:T(128)S(1)} %fusion.156, f32[48,128,256]{2,1,0:T(8,128)} %bitcast.115), kind=kCustom, calls=%fused_computation.3.clone.1 | custom fusion | flops 1572864 | bytes 18874560 | tf_op jit(solution)/shard_map/while/body/eval_jaxpr/scatter-add | solution.py:106
  373.4 7.1 %fusion.166 = bf16[4,128,64]{1,2,0:T(8,128)(2,1)S(1)} fusion(f32[4,128,1536]{2,1,0:T(8,128)} %fusion.163, f32[4,128]{1,0:T(4,128)S(1)} %dynamic-slice_bitcast_fusion.2, bf16[4,1536,256]{1,2,0:T(8,128)(2,1)} %copy-done.2, f32[4,128,1536]{2,1,0:T(8,128)} %get-tuple-element.167, f32[4,128]{1,0:T(4,128)S(1)} %get-tuple-element.168), kind=kOutput, calls=%fused_computation.42.clone.1 | convolution fusion | flops 106203136 | bytes 13441024 | tf_op jit(solution)/shard_map/while/body/eval_jaxpr/gij,gjd->gid/dot_general | solution.py:94
  380.5 8.5 %fusion.164 = f32[4,1536,64]{1,2,0:T(8,128)} fusion(f32[4,128,1536]{2,1,0:T(8,128)} %fusion.163, f32[4,128]{1,0:T(4,128)S(1)} %dynamic-slice_bitcast_fusion.2, bf16[4,128,128]{2,1,0:T(8,128)(2,1)S(1)} %bitcast.128, f32[4,128,1536]{2,1,0:T(8,128)} %get-tuple-element.167, f32[4,128]{1,0:T(4,128)S(1)} %get-tuple-element.168), kind=kOutput, calls=%fused_computation.31.clone.1 | convolution fusion | flops 106170368 | bytes 14292992 | tf_op jit(solution)/shard_map/while/body/eval_jaxpr/gij,gid->gjd/dot_general | solution.py:97
  396.3 7.2 %fusion.165 = bf16[4,128,64]{1,2,0:T(8,128)(2,1)S(1)} fusion(f32[4,128,1536]{2,1,0:T(8,128)} %fusion.161, f32[4,128]{1,0:T(4,128)S(1)} %dynamic-slice_bitcast_fusion.2, bf16[4,1536,256]{1,2,0:T(8,128)(2,1)} %copy-done.2, f32[4,128,1536]{2,1,0:T(8,128)} %get-tuple-element.165, f32[4,128]{1,0:T(4,128)S(1)} %get-tuple-element.166), kind=kOutput, calls=%fused_computation.43.clone.1 | convolution fusion | flops 106203136 | bytes 13441024 | tf_op jit(solution)/shard_map/while/body/eval_jaxpr/gij,gjd->gid/dot_general | solution.py:94
  403.5 8.7 %fusion.162 = f32[4,1536,64]{1,2,0:T(8,128)} fusion(f32[4,128,1536]{2,1,0:T(8,128)} %fusion.161, f32[4,128]{1,0:T(4,128)S(1)} %dynamic-slice_bitcast_fusion.2, bf16[4,128,128]{2,1,0:T(8,128)(2,1)S(1)} %bitcast.130, f32[4,128,1536]{2,1,0:T(8,128)} %get-tuple-element.165, f32[4,128]{1,0:T(4,128)S(1)} %get-tuple-element.166), kind=kOutput, calls=%fused_computation.29.clone.1 | convolution fusion | flops 106170368 | bytes 14292992 | tf_op jit(solution)/shard_map/while/body/eval_jaxpr/gij,gid->gjd/dot_general | solution.py:97
  418.3 6.6 %copy.142 = f32[4,1536,256]{2,1,0:T(8,128)} copy(f32[4,1536,256]{1,2,0:T(8,128)} %pad_maximum_fusion.6) | data formatting | bytes 12582912 | tf_op jit(solution)/shard_map/while/body/eval_jaxpr/concatenate | solution.py:103
  424.9 14.8 %scatter_fusion = f32[32,128,256]{2,1,0:T(8,128)} fusion(f32[32,128,256]{2,1,0:T(8,128)} %get-tuple-element.185, s32[48]{0:T(128)S(1)} %fusion.156, f32[48,128,256]{2,1,0:T(8,128)} %bitcast.115), kind=kCustom, calls=%fused_computation.3.clone.1 | custom fusion | flops 1572864 | bytes 18874560 | tf_op jit(solution)/shard_map/while/body/eval_jaxpr/scatter-add | solution.py:106
  442.3 16.7 %all_to_all.118 = bf16[16,128,256]{2,1,0:T(8,128)(2,1)S(1)} all-to-all(bf16[16,128,256]{2,1,0:T(8,128)(2,1)S(1)} %slice.109), channel_id=1, replica_groups=mesh['dom'=4,'head'=8] {'dom'}, dimensions={0} | all-to-all | bytes 2097152 | tf_op jit(solution)/shard_map/all_to_all | solution.py:113
  469.0 8.8 %all-to-all-done.4 = bf16[8,256,128]{2,1,0:T(8,128)(2,1)S(1)} async-done(((bf16[8,256,128]{2,1,0:T(8,128)(2,1)}), bf16[8,256,128]{2,1,0:T(8,128)(2,1)S(1)}, u32[]{:S(2)}, u32[]{:S(2)}) %all-to-all-start.4) | async-done | bytes 524320 | tf_op jit(solution)/shard_map/all_to_all | solution.py:123
  482.2 14.3 %all-to-all-done.7 = bf16[8,256,128]{2,1,0:T(8,128)(2,1)S(1)} async-done(((bf16[8,256,128]{2,1,0:T(8,128)(2,1)}), bf16[8,256,128]{2,1,0:T(8,128)(2,1)S(1)}, u32[]{:S(2)}, u32[]{:S(2)}) %all-to-all-start.7) | async-done | bytes 524320 | tf_op jit(solution)/shard_map/all_to_all | solution.py:125
  502.5 12.8 %all-to-all-done.6 = bf16[8,256,128]{2,1,0:T(8,128)(2,1)S(1)} async-done(((bf16[8,256,128]{2,1,0:T(8,128)(2,1)}), bf16[8,256,128]{2,1,0:T(8,128)(2,1)S(1)}, u32[]{:S(2)}, u32[]{:S(2)}) %all-to-all-start.6) | async-done | bytes 524320 | tf_op jit(solution)/shard_map/all_to_all | solution.py:124
  (216 shorter events, 211.3 us)
Async XLA Ops:
  0.6 20.2 %copy-start.8 = (bf16[256,1024]{1,0:T(8,128)(2,1)S(1)}, bf16[256,1024]{1,0:T(8,128)(2,1)}, u32[]{:S(2)}) copy-start(bf16[256,1024]{1,0:T(8,128)(2,1)} %param.11) | copy-start | bytes 1572868
  2.6 26.4 %copy-start.12 = (s32[2048]{0:T(1024)S(1)}, s32[2048]{0:T(1024)}, u32[]{:S(2)}) copy-start(s32[2048]{0:T(1024)} %param.13) | copy-start | bytes 24580
  2.6 27.1 %copy-start.9 = (bf16[256,1024]{1,0:T(8,128)(2,1)S(1)}, bf16[256,1024]{1,0:T(8,128)(2,1)}, u32[]{:S(2)}) copy-start(bf16[256,1024]{1,0:T(8,128)(2,1)} %param.9) | copy-start | bytes 1572868
  2.6 22.3 %all-to-all-start.1 = ((bf16[256,8,128]{2,0,1:T(8,128)(2,1)}), bf16[256,8,128]{2,0,1:T(8,128)(2,1)S(1)}, u32[]{:S(2)}, u32[]{:S(2)}) async-start(bf16[256,8,128]{2,0,1:T(8,128)(2,1)} %copy_bitcast_fusion.2), calls=%async_computation.1 | async-start | bytes 1048576 | tf_op jit(solution)/shard_map/all_to_all | solution.py:53
  11.1 38.3 %collective-permute-start = (bf16[256,128]{1,0:T(8,128)(2,1)}, bf16[256,128]{1,0:T(8,128)(2,1)}, u32[]{:S(2)}, u32[]{:S(2)}) collective-permute-start(bf16[256,128]{1,0:T(8,128)(2,1)} %bitcast.17), channel_id=1, source_target_pairs={{0,1},{1,0},{2,3},{3,2},{4,5},{5,4},{6,7},{7,6},{8,9},{9,8},{10,11... | collective-permute-start | bytes 196616 | tf_op jit(solution)/shard_map/ppermute | solution.py:31
  12.3 39.3 %collective-permute-start.1 = (bf16[256,128]{1,0:T(8,128)(2,1)}, bf16[256,128]{1,0:T(8,128)(2,1)}, u32[]{:S(2)}, u32[]{:S(2)}) collective-permute-start(bf16[256,128]{1,0:T(8,128)(2,1)} %bitcast.19), channel_id=1, source_target_pairs={{0,2},{1,3},{2,0},{3,1},{4,6},{5,7},{6,4},{7,5},{8,10},{9,11},{10,... | collective-permute-start | bytes 196616 | tf_op jit(solution)/shard_map/ppermute | solution.py:31
  14.1 39.8 %collective-permute-start.2 = (bf16[256,128]{1,0:T(8,128)(2,1)S(1)}, bf16[256,128]{1,0:T(8,128)(2,1)S(1)}, u32[]{:S(2)}, u32[]{:S(2)}) collective-permute-start(bf16[256,128]{1,0:T(8,128)(2,1)S(1)} %bitcast.141), channel_id=1, source_target_pairs={{0,3},{1,2},{2,1},{3,0},{4,7},{5,6},{6,5},{7,4},{8,11},{9,10},{10,... | collective-permute-start | bytes 196616 | tf_op jit(solution)/shard_map/ppermute | solution.py:31
  14.3 52.8 %collective-permute-start.3 = (bf16[256,128]{1,0:T(8,128)(2,1)S(1)}, bf16[256,128]{1,0:T(8,128)(2,1)S(1)}, u32[]{:S(2)}, u32[]{:S(2)}) collective-permute-start(bf16[256,128]{1,0:T(8,128)(2,1)S(1)} %bitcast.140), channel_id=1, source_target_pairs={{0,4},{1,5},{2,6},{3,7},{4,0},{5,1},{6,2},{7,3},{8,12},{9,13},{10,... | collective-permute-start | bytes 196616 | tf_op jit(solution)/shard_map/ppermute | solution.py:31
  17.1 50.0 %collective-permute-start.4 = (bf16[256,128]{1,0:T(8,128)(2,1)S(1)}, bf16[256,128]{1,0:T(8,128)(2,1)S(1)}, u32[]{:S(2)}, u32[]{:S(2)}) collective-permute-start(bf16[256,128]{1,0:T(8,128)(2,1)S(1)} %bitcast.139), channel_id=1, source_target_pairs={{0,5},{1,4},{2,7},{3,6},{4,1},{5,0},{6,3},{7,2},{8,13},{9,12},{10,... | collective-permute-start | bytes 196616 | tf_op jit(solution)/shard_map/ppermute | solution.py:31
  18.1 10.3 %copy-start.13 = (s32[16]{0:T(128)}, s32[16]{0:T(128)S(1)}, u32[]{:S(2)}) copy-start(s32[16]{0:T(128)S(1)} %max.25) | copy-start | bytes 196
  24.9 18.8 %all-to-all-start.2 = ((bf16[256,8,128]{2,0,1:T(8,128)(2,1)}), bf16[256,8,128]{2,0,1:T(8,128)(2,1)S(1)}, u32[]{:S(2)}, u32[]{:S(2)}) async-start(bf16[256,8,128]{2,0,1:T(8,128)(2,1)} %copy_bitcast_fusion.1), calls=%async_computation.2 | async-start | bytes 1048576 | tf_op jit(solution)/shard_map/all_to_all | solution.py:54
  29.0 15.6 %copy-start.15 = (pred[16]{0:T(512)(128)(4,1)S(1)}, pred[16]{0:T(512)(128)(4,1)}, u32[]{:S(2)}) copy-start(pred[16]{0:T(512)(128)(4,1)} %broadcast_compare_fusion) | copy-start | bytes 52
  43.8 5.7 %copy-start.16 = (s32[8]{0:T(128)S(1)}, s32[8]{0:T(128)}, u32[]{:S(2)}) copy-start(s32[8]{0:T(128)} %fusion.90) | copy-start | bytes 100
  44.5 4.9 copy-start.11
  44.6 6.2 %copy-start.7 = (bf16[8,256,128]{2,1,0:T(8,128)(2,1)S(1)}, bf16[8,256,128]{2,1,0:T(8,128)(2,1)}, u32[]{:S(2)}) copy-start(bf16[8,256,128]{2,1,0:T(8,128)(2,1)} %bitcast_dynamic-update-slice_fusion.8) | copy-start | bytes 1572868
  44.6 7.1 %copy-start.10 = (bf16[256,1,128]{2,0,1:T(8,128)(2,1)S(1)}, bf16[256,1,128]{2,0,1:T(8,128)(2,1)}, u32[]{:S(2)}) copy-start(bf16[256,1,128]{2,0,1:T(8,128)(2,1)} %copy.103) | copy-start | bytes 196612
  45.7 17.2 %all-to-all-start.3 = ((bf16[16,128,256]{2,1,0:T(8,128)(2,1)}), bf16[16,128,256]{2,1,0:T(8,128)(2,1)S(1)}, u32[]{:S(2)}, u32[]{:S(2)}) async-start(bf16[16,128,256]{2,1,0:T(8,128)(2,1)} %broadcast_select_fusion.1), calls=%async_computation.3 | async-start | bytes 2097152 | tf_op jit(solution)/shard_map/all_to_all | solution.py:41
  49.5 17.7 %collective-permute-start.5 = (bf16[256,128]{1,0:T(8,128)(2,1)S(1)}, bf16[256,128]{1,0:T(8,128)(2,1)S(1)}, u32[]{:S(2)}, u32[]{:S(2)}) collective-permute-start(bf16[256,128]{1,0:T(8,128)(2,1)S(1)} %bitcast.143), channel_id=1, source_target_pairs={{0,6},{1,7},{2,4},{3,5},{4,2},{5,3},{6,0},{7,1},{8,14},{9,15},{10,... | collective-permute-start | bytes 196616 | tf_op jit(solution)/shard_map/ppermute | solution.py:31
  51.7 15.5 %collective-permute-start.6 = (bf16[256,128]{1,0:T(8,128)(2,1)S(1)}, bf16[256,128]{1,0:T(8,128)(2,1)S(1)}, u32[]{:S(2)}, u32[]{:S(2)}) collective-permute-start(bf16[256,128]{1,0:T(8,128)(2,1)S(1)} %bitcast.142), channel_id=1, source_target_pairs={{0,7},{1,6},{2,5},{3,4},{4,3},{5,2},{6,1},{7,0},{8,15},{9,14},{10,... | collective-permute-start | bytes 196616 | tf_op jit(solution)/shard_map/ppermute | solution.py:31
  62.9 4.3 copy-start.6
  62.9 19.5 %all-to-all-start = ((bf16[256,8,128]{2,0,1:T(8,128)(2,1)}), bf16[256,8,128]{2,0,1:T(8,128)(2,1)}, u32[]{:S(2)}, u32[]{:S(2)}) async-start(bf16[256,8,128]{2,0,1:T(8,128)(2,1)} %copy_bitcast_fusion.3), calls=%async_computation | async-start | bytes 1048576 | tf_op jit(solution)/shard_map/all_to_all | solution.py:52
  145.5 2.8 copy-start.4
  145.5 3.3 copy-start.5
  234.5 2.8 copy-start.4
  234.5 3.3 copy-start.5
  323.3 3.3 copy-start.5
  412.2 3.3 copy-start.5
  459.0 18.8 %all-to-all-start.4 = ((bf16[8,256,128]{2,1,0:T(8,128)(2,1)}), bf16[8,256,128]{2,1,0:T(8,128)(2,1)S(1)}, u32[]{:S(2)}, u32[]{:S(2)}) async-start(bf16[8,256,128]{2,1,0:T(8,128)(2,1)} %bitcast.33), calls=%async_computation.4 | async-start | bytes 1048576 | tf_op jit(solution)/shard_map/all_to_all | solution.py:123
  462.5 4.6 copy-start.14
  477.8 18.8 %all-to-all-start.7 = ((bf16[8,256,128]{2,1,0:T(8,128)(2,1)}), bf16[8,256,128]{2,1,0:T(8,128)(2,1)S(1)}, u32[]{:S(2)}, u32[]{:S(2)}) async-start(bf16[8,256,128]{2,1,0:T(8,128)(2,1)} %bitcast.41), calls=%async_computation.7 | async-start | bytes 1048576 | tf_op jit(solution)/shard_map/all_to_all | solution.py:125
  496.6 18.8 %all-to-all-start.6 = ((bf16[8,256,128]{2,1,0:T(8,128)(2,1)}), bf16[8,256,128]{2,1,0:T(8,128)(2,1)S(1)}, u32[]{:S(2)}, u32[]{:S(2)}) async-start(bf16[8,256,128]{2,1,0:T(8,128)(2,1)} %bitcast.38), calls=%async_computation.6 | async-start | bytes 1048576 | tf_op jit(solution)/shard_map/all_to_all | solution.py:124
  500.1 16.5 %copy-start.1 = (bf16[256,1024]{1,0:T(8,128)(2,1)S(1)}, bf16[256,1024]{1,0:T(8,128)(2,1)}, u32[]{:S(2)}) copy-start(bf16[256,1024]{1,0:T(8,128)(2,1)} %param.10) | copy-start | bytes 1572868
  (11 other events, 27.5 us)
